TPU v7x, 256 devices: a whole 4x4x8 slice. The times are simulated.
256 devices in a mesh: fib: 8 (over y, x_hi), rest: 32 (over z, x_lo, core).
Axes of the slice: x: 4 (x_hi: 2, x_lo: 2; x = x_hi * 2 + x_lo), y: 4, z: 8, core: 2. Of those that a mesh axis runs over, the one named last changes fastest.
Arguments:
- tensor: float32 [64, 128, 64, 1024], P('fib', 'rest'), may hold values from -24 to 24
- factor_one: float32 [1024, 128], replicated, may hold values from 0 to 0.05
- factor_two: float32 [64, 128], P('fib'), may hold values from 0.05 to 0.35
- factor_three: float32 [128, 128], P('rest'), may hold values from 0.03 to 0.25
- factor_four: float32 [64, 128], replicated, may hold values from 0.03 to 0.25
Outputs:
- new_factor: float32 [1024, 128], replicated
- factor_gram: float32 [128, 128], replicated
All inputs are finite; a program needn't handle non-finite values.
Results may differ from a plain program's by a relative error of at most 0.00014.
Values sent between devices are 32-bit elements; how exact they have to be, the bound alone decides.
No kernel may reach another device: no remote copies, remote signals or barrier semaphores. Data moves between devices by JAX's collectives and lax.ppermute only.
A program may use at most 64 MiB of HBM per device.

v0:
```python
import jax
import jax.numpy as jnp
from jax import lax
from jax.sharding import PartitionSpec as P


def from_everyone(value, axis):
    size = lax.axis_size(axis)
    return lax.all_to_all(
        jnp.broadcast_to(value[None], (size, *value.shape)), axis, 0, 0, tiled=True
    )


def of_everyone(value, axis):
    everything = from_everyone(value, axis)
    return jnp.sum(everything, axis=0)


def gathered_total(value, axis):
    return lax.all_gather(value, axis).sum(0)


def hals_columns(factor, mttkrp, gram_v):
    highest = lax.Precision.HIGHEST
    rank_cols = factor.shape[1]
    width = 16
    current = factor
    for block_idx in range(rank_cols // width):
        lower = block_idx * width
        base = jnp.dot(current, gram_v[:, lower : lower + width], precision=highest)
        old_cols = current[:, lower : lower + width]
        inner = gram_v[lower : lower + width, lower : lower + width]
        target = mttkrp[:, lower : lower + width]

        def update(k, cols):
            index = k.astype(jnp.int32)
            zero = jnp.zeros((), jnp.int32)
            inner_col = lax.dynamic_slice_in_dim(inner, index, 1, 1)
            diag = lax.dynamic_slice_in_dim(inner_col, index, 1, 0)[0, 0]
            product = (
                lax.dynamic_slice_in_dim(base, index, 1, 1)[:, 0]
                + jnp.dot(cols - old_cols, inner_col, precision=highest)[:, 0]
            )
            goal = lax.dynamic_slice_in_dim(target, index, 1, 1)[:, 0]
            column = lax.dynamic_slice_in_dim(cols, index, 1, 1)[:, 0]
            fresh = jnp.maximum(column + (goal - product) / diag, 0.0)
            return lax.dynamic_update_slice(cols, fresh[:, None], (zero, index))

        cols = lax.fori_loop(0, width, update, old_cols)
        current = current.at[:, lower : lower + width].set(cols)
    return current


def per_device(tensor, factor_one, factor_two, factor_three, factor_four):
    highest = lax.Precision.HIGHEST
    rank_cols = factor_one.shape[1]
    mode_one = tensor.shape[3]
    khatri = (
        factor_two[:, None, None, :]
        * factor_three[None, :, None, :]
        * factor_four[None, None, :, :]
    ).reshape(-1, rank_cols)
    flat = tensor.reshape(-1, mode_one)
    part_two = jnp.dot(factor_two.T, factor_two, precision=highest)
    part_three = jnp.dot(factor_three.T, factor_three, precision=highest)
    gram_four = jnp.dot(factor_four.T, factor_four, precision=highest)
    gram_two = of_everyone(part_two, "fib")
    gram_three = gathered_total(part_three, "rest")
    gram_v = gram_two * gram_three * gram_four
    partial_value = lax.dot_general(flat, khatri, (((0,), (0,)), ((), ())), precision=highest)
    mttkrp = lax.psum(partial_value, ("fib", "rest"))
    new_factor = hals_columns(factor_one, mttkrp, gram_v)
    factor_gram = jnp.dot(new_factor.T, new_factor, precision=highest)
    return (new_factor, factor_gram)


def solution(mesh):
    return jax.shard_map(
        per_device,
        mesh=mesh,
        in_specs=(P("fib", "rest", None, None), P(), P("fib", None), P("rest", None), P()),
        out_specs=(P(), P()),
        check_vma=False,
    )
```

profile of v0, /device:TPU:2, one launch (start us, length us, event | category | flops | bytes accessed | tf_op | source)
XLA Modules:
  0.0 526.8 jit_solution(3609673047529688155)
XLA Ops:
  8.1 1.0 copy.149
  9.8 7.8 %convolution_bitcast_fusion.8 = f32[1024,128]{0,1:T(8,128)} fusion(f32[8,4,64,1024]{3,2,1,0:T(8,128)} %param.37, f32[64,128]{1,0:T(8,128)} %param.41, f32[8,4,128]{2,1,0:T(4,128)S(1)} %broadcast_multiply_fusion), kind=kOutput, calls=%fused_computation.64 | convolution fusion | flops 3221487616 | bytes 8962048 | tf_op jit(solution)/shard_map/dot_general | solution.py:70
  17.8 0.9 fusion.69
  19.0 0.8 broadcast_in_dim.33
  19.9 6.0 %all-to-all-start = ((f32[8,128,128]{2,1,0:T(8,128)}), f32[8,128,128]{2,1,0:T(8,128)S(1)}, u32[]{:S(2)}, u32[]{:S(2)}) async-start(f32[8,128,128]{2,1,0:T(8,128)} %broadcast_in_dim.33), calls=%async_computation | async-start | bytes 1048576 | tf_op jit(solution)/shard_map/all_to_all | solution.py:9
  30.8 246.9 %all-reduce.2.cloned.1.call-done = f32[1024,128]{0,1:T(8,128)} async-done(((f32[1024,128]{0,1:T(8,128)}), f32[1024,128]{0,1:T(8,128)}) %all-reduce.2.cloned.1.call-update) | async-done | bytes 524304 | tf_op jit(solution)/shard_map/psum | solution.py:71
  277.7 1.1 fusion.66
  279.0 1.7 reduce_sum.19
  281.7 24.8 %while.136 = (s32[]{:T(128)}, f32[1024,16]{0,1:T(8,128)S(1)}, f32[1024,16]{0,1:T(8,128)S(1)}, f32[1024,16]{0,1:T(8,128)S(1)}, f32[1024,16]{0,1:T(8,128)S(1)}, /*...) while((s32[]{:T(128)}, f32[1024,16]{0,1:T(8,128)S(1)}, f32[1024,16]{0,1:T(8,128)S(1)}, ...), condition=%wide.region_5.0_spmd, body=%wide.region_4.0_spmd.sunk | while | flops 218115 | bytes 157821 | solution.py:49
  282.3 0.8 fusion.105
  283.8 0.8 fusion.105
  285.4 0.8 fusion.105
  286.9 0.8 fusion.105
  288.5 0.8 fusion.105
  290.0 0.8 fusion.105
  291.6 0.8 fusion.105
  293.1 0.8 fusion.105
  294.7 0.8 fusion.105
  296.2 0.8 fusion.105
  297.8 0.8 fusion.105
  299.3 0.8 fusion.105
  300.9 0.8 fusion.105
  302.4 0.8 fusion.105
  304.0 0.8 fusion.105
  305.6 0.8 fusion.105
  307.4 2.3 scatter.26
  310.6 24.8 %while.137 = (s32[]{:T(128)}, f32[1024,16]{0,1:T(8,128)S(1)}, f32[1024,16]{0,1:T(8,128)S(1)}, f32[1024,16]{0,1:T(8,128)S(1)}, f32[1024,16]{0,1:T(8,128)S(1)}, /*...) while((s32[]{:T(128)}, f32[1024,16]{0,1:T(8,128)S(1)}, f32[1024,16]{0,1:T(8,128)S(1)}, ...), condition=%wide.region_8.0_spmd, body=%wide.region_7.0_spmd.sunk | while | flops 218115 | bytes 157821 | solution.py:49
  319.0 0.8 fusion.107
  320.5 0.8 fusion.107
  323.6 0.8 fusion.107
  325.2 0.8 fusion.107
  328.3 0.8 fusion.107
  329.8 0.8 fusion.107
  332.9 0.8 fusion.107
  334.4 0.8 fusion.107
  335.6 0.8 broadcast_select_fusion.5
  336.4 3.1 scatter.29
  340.4 24.8 %while.138 = (s32[]{:T(128)}, f32[1024,16]{0,1:T(8,128)S(1)}, f32[1024,16]{0,1:T(8,128)S(1)}, f32[1024,16]{0,1:T(8,128)S(1)}, f32[1024,16]{0,1:T(8,128)S(1)}, /*...) while((s32[]{:T(128)}, f32[1024,16]{0,1:T(8,128)S(1)}, f32[1024,16]{0,1:T(8,128)S(1)}, ...), condition=%wide.region_11.0_spmd, body=%wide.region_10.0_spmd.sunk | while | flops 218115 | bytes 157821 | solution.py:49
  351.9 0.8 fusion.109
  355.0 0.8 fusion.109
  356.5 0.8 fusion.109
  359.6 0.8 fusion.109
  361.2 0.8 fusion.109
  362.7 0.8 fusion.109
  364.3 0.8 fusion.109
  365.4 0.8 broadcast_select_fusion.4
  366.3 3.1 scatter.30
  370.3 24.7 %while.139 = (s32[]{:T(128)}, f32[1024,16]{0,1:T(8,128)S(1)}, f32[1024,16]{0,1:T(8,128)S(1)}, f32[1024,16]{0,1:T(8,128)S(1)}, f32[1024,16]{0,1:T(8,128)S(1)}, /*...) while((s32[]{:T(128)}, f32[1024,16]{0,1:T(8,128)S(1)}, f32[1024,16]{0,1:T(8,128)S(1)}, ...), condition=%wide.region_14.0_spmd, body=%wide.region_13.0_spmd.sunk | while | flops 218115 | bytes 157821 | solution.py:49
  391.0 0.8 fusion.111
  392.5 0.8 fusion.111
  396.0 3.1 scatter.31
  400.0 24.8 %while.140 = (s32[]{:T(128)}, f32[1024,16]{0,1:T(8,128)S(1)}, f32[1024,16]{0,1:T(8,128)S(1)}, f32[1024,16]{0,1:T(8,128)S(1)}, f32[1024,16]{0,1:T(8,128)S(1)}, /*...) while((s32[]{:T(128)}, f32[1024,16]{0,1:T(8,128)S(1)}, f32[1024,16]{0,1:T(8,128)S(1)}, ...), condition=%wide.region_17.0_spmd, body=%wide.region_16.0_spmd.sunk | while | flops 218115 | bytes 157821 | solution.py:49
  417.6 0.8 fusion.113
  419.1 0.8 fusion.113
  425.0 0.9 broadcast_select_fusion.2
  425.8 3.1 scatter.34
  429.8 24.7 %while.141 = (s32[]{:T(128)}, f32[1024,16]{0,1:T(8,128)S(1)}, f32[1024,16]{0,1:T(8,128)S(1)}, f32[1024,16]{0,1:T(8,128)S(1)}, f32[1024,16]{0,1:T(8,128)S(1)}, /*...) while((s32[]{:T(128)}, f32[1024,16]{0,1:T(8,128)S(1)}, f32[1024,16]{0,1:T(8,128)S(1)}, ...), condition=%wide.region_20.0_spmd, body=%wide.region_19.0_spmd.sunk | while | flops 218115 | bytes 157821 | solution.py:49
  455.6 3.1 scatter.35
  459.6 24.7 %while.142 = (s32[]{:T(128)}, f32[1024,16]{0,1:T(8,128)S(1)}, f32[1024,16]{0,1:T(8,128)S(1)}, f32[1024,16]{0,1:T(8,128)S(1)}, f32[1024,16]{0,1:T(8,128)S(1)}, /*...) while((s32[]{:T(128)}, f32[1024,16]{0,1:T(8,128)S(1)}, f32[1024,16]{0,1:T(8,128)S(1)}, ...), condition=%wide.region_23.0_spmd, body=%wide.region_22.0_spmd.sunk | while | flops 218115 | bytes 157821 | solution.py:49
  484.5 0.9 broadcast_select_fusion
  485.4 3.3 scatter.36
  489.6 24.8 %while.143 = (s32[]{:T(128)}, f32[1024,16]{0,1:T(8,128)S(1)}, f32[1024,16]{0,1:T(8,128)S(1)}, f32[1024,16]{0,1:T(8,128)S(1)}, f32[1024,16]{0,1:T(8,128)S(1)}, /*...) while((s32[]{:T(128)}, f32[1024,16]{0,1:T(8,128)S(1)}, f32[1024,16]{0,1:T(8,128)S(1)}, ...), condition=%wide.region_25.0_spmd, body=%wide.region_24.0_spmd.sunk | while | flops 218115 | bytes 157821 | solution.py:49
  514.6 3.1 scatter.39
  517.7 1.6 fusion.70
  (419 shorter events, 182.7 us)
Async XLA Ops:
  8.0 10.7 %copy-start.2 = (f32[8,128]{1,0:T(8,128)S(1)}, f32[8,128]{1,0:T(8,128)}, u32[]{:S(2)}) copy-start(f32[8,128]{1,0:T(8,128)} %param.39) | copy-start | bytes 12292
  8.0 9.7 %copy-start.3 = (f32[4,128]{1,0:T(4,128)S(1)}, f32[4,128]{1,0:T(4,128)}, u32[]{:S(2)}) copy-start(f32[4,128]{1,0:T(4,128)} %param.40) | copy-start | bytes 6148
  8.0 272.8 %copy-start.1 = (f32[64,128]{1,0:T(8,128)S(1)}, f32[64,128]{1,0:T(8,128)}, u32[]{:S(2)}) copy-start(f32[64,128]{1,0:T(8,128)} %param.41) | copy-start | bytes 98308
  8.0 269.7 %all-reduce.2.cloned.1.call-start = ((), (), s32[]{:S(2)}) async-start(), calls=%async_computation.1 | async-start | bytes 1048576 | tf_op jit(solution)/shard_map/psum | solution.py:71
  17.7 261.3 %all-gather.3.cloned.1.call-start = ((), (), s32[]{:S(2)}) async-start(), calls=%async_computation.2 | async-start | bytes 2162688 | tf_op jit(solution)/shard_map/all_gather | solution.py:20
  19.9 258.9 %all-to-all-start = ((f32[8,128,128]{2,1,0:T(8,128)}), f32[8,128,128]{2,1,0:T(8,128)S(1)}, u32[]{:S(2)}, u32[]{:S(2)}) async-start(f32[8,128,128]{2,1,0:T(8,128)} %broadcast_in_dim.33), calls=%async_computation | async-start | bytes 1048576 | tf_op jit(solution)/shard_map/all_to_all | solution.py:9
  517.7 1.7 copy-start
Sparse Core Ops, SparseCore 0:
  17.8 259.8 all-reduce.1
Sparse Core Ops, SparseCore 1:
  20.6 66.9 all-gather.2
where the time goes:
time: 528 us; the launch traced here: 527 us
  waiting for transfers between devices  247 us (47%)
  local copies, waits for them, and re-layouts  121 us (23%)
  matrix products  120 us (23%)
  between operations  15.8 us (3%)
  other arithmetic  12.8 us (2%)
  starting transfers between devices  6.11 us (1%)
    psum x1, waiting for transfers between devices, per_device(): mttkrp = lax.psum(partial_value, ('fib', 'rest'))  247 us
    dot_general x128, matrix products, update(): jnp.dot(cols - old_cols, inner_col, precision=highest)[:, 0]  104 us
    dynamic_slice x128, local copies, waits for them, and re-layouts, update(): diag = lax.dynamic_slice_in_dim(inner_col, index, 1, 0)[0, 0]  75.3 us
    scatter x8, local copies, waits for them, and re-layouts, hals_columns(): current = current.at[:, lower:lower + width].set(cols)  23.9 us
    dynamic_update_slice x128, local copies, waits for them, and re-layouts, update(): return lax.dynamic_update_slice(cols, fresh[:, None], (zero, index))  14.1 us
  transfers between devices with their start and end apart: 3, of which 1 were waited for; matrix products, arithmetic and copies ran while one was open for 2% of the time, Pallas kernels for 0%

commit v1 on v0

--- a/solution.py
+++ b/solution.py
@@ -68,7 +68,7 @@
     gram_three = gathered_total(part_three, "rest")
     gram_v = gram_two * gram_three * gram_four
     partial_value = lax.dot_general(flat, khatri, (((0,), (0,)), ((), ())), precision=highest)
-    mttkrp = lax.psum(partial_value, ("fib", "rest"))
+    mttkrp = lax.psum(lax.psum(partial_value, "fib"), "rest")
     new_factor = hals_columns(factor_one, mttkrp, gram_v)
     factor_gram = jnp.dot(new_factor.T, new_factor, precision=highest)
     return (new_factor, factor_gram)

time: 528 us -> 657 us (1.24)
  waiting for transfers between devices: 247 us -> 377 us
    all_gather x1, waiting for transfers between devices: 0.03 us -> 69.1 us  [gathered_total(): return lax.all_gather(value, axis).sum(0)]
    psum x1 -> x2, waiting for transfers between devices: 247 us -> 303 us  [per_device(): mttkrp = lax.psum(lax.psum(partial_value, 'fib'), 'rest')]
  transfers between devices with their start and end apart: 3 -> 4, of which waited for: 1 -> 4; matrix products, arithmetic and copies ran while one was open for 2% -> 1% of each run, Pallas kernels for 0% -> 0%
where the time goes in v1:
time: 657 us; the launch traced here: 653 us
  waiting for transfers between devices  377 us (57%)
  local copies, waits for them, and re-layouts  121 us (18%)
  matrix products  120 us (18%)
  between operations  14.1 us (2%)
  other arithmetic  12.8 us (2%)
    psum x2, waiting for transfers between devices, per_device(): mttkrp = lax.psum(lax.psum(partial_value, 'fib'), 'rest')  303 us
    dot_general x128, matrix products, update(): jnp.dot(cols - old_cols, inner_col, precision=highest)[:, 0]  104 us
    dynamic_slice x128, local copies, waits for them, and re-layouts, update(): diag = lax.dynamic_slice_in_dim(inner_col, index, 1, 0)[0, 0]  75.3 us
    all_gather x1, waiting for transfers between devices, gathered_total(): return lax.all_gather(value, axis).sum(0)  69.1 us
    scatter x8, local copies, waits for them, and re-layouts, hals_columns(): current = current.at[:, lower:lower + width].set(cols)  23.9 us
    dynamic_update_slice x128, local copies, waits for them, and re-layouts, update(): return lax.dynamic_update_slice(cols, fresh[:, None], (zero, index))  14.1 us
  transfers between devices with their start and end apart: 4, of which 4 were waited for; matrix products, arithmetic and copies ran while one was open for 1% of the time, Pallas kernels for 0%

profile of v1, /device:TPU:2, one launch (start us, length us, event | category | flops | bytes accessed | tf_op | source)
XLA Modules:
  0.0 653.2 jit_solution(8107987271859167956)
XLA Ops:
  7.2 1.0 copy.150
  9.0 7.8 %convolution_bitcast_fusion.8 = f32[1024,128]{0,1:T(8,128)} fusion(f32[8,4,64,1024]{3,2,1,0:T(8,128)} %param.37, f32[64,128]{1,0:T(8,128)} %param.41, f32[8,4,128]{2,1,0:T(4,128)S(1)} %broadcast_multiply_fusion), kind=kOutput, calls=%fused_computation.64 | convolution fusion | flops 3221487616 | bytes 8962048 | tf_op jit(solution)/shard_map/dot_general | solution.py:70
  16.9 93.7 %all-reduce.3.cloned.1.call-done = f32[1024,128]{0,1:T(8,128)} async-done(((f32[1024,128]{0,1:T(8,128)}), f32[1024,128]{0,1:T(8,128)}) %all-reduce.3.cloned.1.call-update) | async-done | bytes 524304 | tf_op jit(solution)/shard_map/psum | solution.py:71
  110.7 0.9 fusion.69
  112.0 0.8 broadcast_in_dim.33
  112.8 3.7 all-to-all-start
  121.4 5.1 all-to-all-done
  126.6 209.4 %all-reduce.5.cloned.1.call-done = f32[1024,128]{0,1:T(8,128)} async-done(((f32[1024,128]{0,1:T(8,128)}), f32[1024,128]{0,1:T(8,128)}) %all-reduce.5.cloned.1.call-update) | async-done | bytes 524304 | tf_op jit(solution)/shard_map/psum | solution.py:71
  336.0 1.1 fusion.66
  337.1 69.1 %all-gather.3.cloned.1.call-done = f32[4096,128]{1,0:T(8,128)} async-done(((f32[128,128]{1,0:T(8,128)}), f32[4096,128]{1,0:T(8,128)}) %all-gather.3.cloned.1.call-update) | async-done | bytes 2097168 | tf_op jit(solution)/shard_map/all_gather | solution.py:20
  406.3 1.7 reduce_sum.19
  409.0 24.8 %while.136 = (s32[]{:T(128)}, f32[1024,16]{0,1:T(8,128)S(1)}, f32[1024,16]{0,1:T(8,128)S(1)}, f32[1024,16]{0,1:T(8,128)S(1)}, f32[1024,16]{0,1:T(8,128)S(1)}, /*...) while((s32[]{:T(128)}, f32[1024,16]{0,1:T(8,128)S(1)}, f32[1024,16]{0,1:T(8,128)S(1)}, ...), condition=%wide.region_6.0_spmd, body=%wide.region_5.0_spmd.sunk | while | flops 218115 | bytes 157821 | solution.py:49
  409.6 0.8 fusion.105
  411.1 0.8 fusion.105
  412.7 0.8 fusion.105
  414.2 0.8 fusion.105
  415.8 0.8 fusion.105
  417.3 0.8 fusion.105
  418.9 0.8 fusion.105
  420.4 0.8 fusion.105
  422.0 0.8 fusion.105
  423.5 0.8 fusion.105
  425.1 0.8 fusion.105
  426.6 0.8 fusion.105
  428.2 0.8 fusion.105
  429.7 0.8 fusion.105
  431.3 0.8 fusion.105
  432.8 0.8 fusion.105
  434.7 2.3 scatter.26
  437.9 24.8 %while.137 = (s32[]{:T(128)}, f32[1024,16]{0,1:T(8,128)S(1)}, f32[1024,16]{0,1:T(8,128)S(1)}, f32[1024,16]{0,1:T(8,128)S(1)}, f32[1024,16]{0,1:T(8,128)S(1)}, /*...) while((s32[]{:T(128)}, f32[1024,16]{0,1:T(8,128)S(1)}, f32[1024,16]{0,1:T(8,128)S(1)}, ...), condition=%wide.region_9.0_spmd, body=%wide.region_8.0_spmd.sunk | while | flops 218115 | bytes 157821 | solution.py:49
  443.1 0.8 fusion.107
  444.7 0.8 fusion.107
  446.2 0.8 fusion.107
  447.8 0.8 fusion.107
  449.3 0.8 fusion.107
  450.9 0.8 fusion.107
  454.0 0.8 fusion.107
  455.5 0.8 fusion.107
  458.6 0.8 fusion.107
  460.2 0.8 fusion.107
  462.9 0.8 broadcast_select_fusion.5
  463.7 3.1 scatter.29
  467.7 24.8 %while.138 = (s32[]{:T(128)}, f32[1024,16]{0,1:T(8,128)S(1)}, f32[1024,16]{0,1:T(8,128)S(1)}, f32[1024,16]{0,1:T(8,128)S(1)}, f32[1024,16]{0,1:T(8,128)S(1)}, /*...) while((s32[]{:T(128)}, f32[1024,16]{0,1:T(8,128)S(1)}, f32[1024,16]{0,1:T(8,128)S(1)}, ...), condition=%wide.region_12.0_spmd, body=%wide.region_11.0_spmd.sunk | while | flops 218115 | bytes 157821 | solution.py:49
  480.7 0.8 fusion.109
  482.3 0.8 fusion.109
  485.4 0.8 fusion.109
  486.9 0.8 fusion.109
  490.0 0.8 fusion.109
  491.6 0.8 fusion.109
  492.7 0.8 broadcast_select_fusion.4
  493.5 3.1 scatter.30
  497.5 24.7 %while.139 = (s32[]{:T(128)}, f32[1024,16]{0,1:T(8,128)S(1)}, f32[1024,16]{0,1:T(8,128)S(1)}, f32[1024,16]{0,1:T(8,128)S(1)}, f32[1024,16]{0,1:T(8,128)S(1)}, /*...) while((s32[]{:T(128)}, f32[1024,16]{0,1:T(8,128)S(1)}, f32[1024,16]{0,1:T(8,128)S(1)}, ...), condition=%wide.region_15.0_spmd, body=%wide.region_14.0_spmd.sunk | while | flops 218115 | bytes 157821 | solution.py:49
  523.3 3.1 scatter.31
  527.3 24.8 %while.140 = (s32[]{:T(128)}, f32[1024,16]{0,1:T(8,128)S(1)}, f32[1024,16]{0,1:T(8,128)S(1)}, f32[1024,16]{0,1:T(8,128)S(1)}, f32[1024,16]{0,1:T(8,128)S(1)}, /*...) while((s32[]{:T(128)}, f32[1024,16]{0,1:T(8,128)S(1)}, f32[1024,16]{0,1:T(8,128)S(1)}, ...), condition=%wide.region_18.0_spmd, body=%wide.region_17.0_spmd.sunk | while | flops 218115 | bytes 157821 | solution.py:49
  552.2 0.9 broadcast_select_fusion.2
  553.1 3.1 scatter.34
  557.1 24.7 %while.141 = (s32[]{:T(128)}, f32[1024,16]{0,1:T(8,128)S(1)}, f32[1024,16]{0,1:T(8,128)S(1)}, f32[1024,16]{0,1:T(8,128)S(1)}, f32[1024,16]{0,1:T(8,128)S(1)}, /*...) while((s32[]{:T(128)}, f32[1024,16]{0,1:T(8,128)S(1)}, f32[1024,16]{0,1:T(8,128)S(1)}, ...), condition=%wide.region_21.0_spmd, body=%wide.region_20.0_spmd.sunk | while | flops 218115 | bytes 157821 | solution.py:49
  582.8 3.1 scatter.35
  586.8 24.7 %while.142 = (s32[]{:T(128)}, f32[1024,16]{0,1:T(8,128)S(1)}, f32[1024,16]{0,1:T(8,128)S(1)}, f32[1024,16]{0,1:T(8,128)S(1)}, f32[1024,16]{0,1:T(8,128)S(1)}, /*...) while((s32[]{:T(128)}, f32[1024,16]{0,1:T(8,128)S(1)}, f32[1024,16]{0,1:T(8,128)S(1)}, ...), condition=%wide.region_24.0_spmd, body=%wide.region_23.0_spmd.sunk | while | flops 218115 | bytes 157821 | solution.py:49
  611.8 0.9 broadcast_select_fusion
  612.7 3.3 scatter.36
  616.9 24.8 %while.143 = (s32[]{:T(128)}, f32[1024,16]{0,1:T(8,128)S(1)}, f32[1024,16]{0,1:T(8,128)S(1)}, f32[1024,16]{0,1:T(8,128)S(1)}, f32[1024,16]{0,1:T(8,128)S(1)}, /*...) while((s32[]{:T(128)}, f32[1024,16]{0,1:T(8,128)S(1)}, f32[1024,16]{0,1:T(8,128)S(1)}, ...), condition=%wide.region_26.0_spmd, body=%wide.region_25.0_spmd.sunk | while | flops 218115 | bytes 157821 | solution.py:49
  641.9 3.1 scatter.39
  645.0 1.6 fusion.70
  (422 shorter events, 185.2 us)
Async XLA Ops:
  7.2 104.5 %copy-start.2 = (f32[8,128]{1,0:T(8,128)S(1)}, f32[8,128]{1,0:T(8,128)}, u32[]{:S(2)}) copy-start(f32[8,128]{1,0:T(8,128)} %param.39) | copy-start | bytes 12292
  7.2 103.5 %copy-start.3 = (f32[4,128]{1,0:T(4,128)S(1)}, f32[4,128]{1,0:T(4,128)}, u32[]{:S(2)}) copy-start(f32[4,128]{1,0:T(4,128)} %param.40) | copy-start | bytes 6148
  7.2 103.5 %all-reduce.3.cloned.1.call-start = ((), (), s32[]{:S(2)}) async-start(), calls=%async_computation.1 | async-start | bytes 1048576 | tf_op jit(solution)/shard_map/psum | solution.py:71
  8.3 399.8 %copy-start.1 = (f32[64,128]{1,0:T(8,128)S(1)}, f32[64,128]{1,0:T(8,128)}, u32[]{:S(2)}) copy-start(f32[64,128]{1,0:T(8,128)} %param.41) | copy-start | bytes 98308
  16.9 319.2 %all-reduce.5.cloned.1.call-start = ((), (), s32[]{:S(2)}) async-start(), calls=%async_computation.2 | async-start | bytes 1048576 | tf_op jit(solution)/shard_map/psum | solution.py:71
  110.7 295.6 %all-gather.3.cloned.1.call-start = ((), (), s32[]{:S(2)}) async-start(), calls=%async_computation.3 | async-start | bytes 2162688 | tf_op jit(solution)/shard_map/all_gather | solution.py:20
  112.8 13.7 %all-to-all-start = ((f32[8,128,128]{2,1,0:T(8,128)}), f32[8,128,128]{2,1,0:T(8,128)S(1)}, u32[]{:S(2)}, u32[]{:S(2)}) async-start(f32[8,128,128]{2,1,0:T(8,128)} %broadcast_in_dim.33), calls=%async_computation | async-start | bytes 1048576 | tf_op jit(solution)/shard_map/all_to_all | solution.py:9
  645.0 1.7 copy-start
Sparse Core Ops, SparseCore 0:
  17.0 93.6 all-reduce.2
  113.3 222.7 all-reduce.4
  338.5 67.7 all-gather.2
